TPU v7x, 256 devices: a whole 4x4x8 slice. The times are simulated.
256 devices in a mesh: row: 8 (over x, core), col: 32 (over y, z).
Axes of the slice: x: 4, y: 4, z: 8, core: 2. Of those that a mesh axis runs over, the one named last changes fastest.
Arguments:
- factor: float32 [6, 8, 32, 512, 512], P(None, 'row', 'col'), may hold values from -0.1875 to 0.1875
- rhs: float32 [6, 8, 32, 128, 128], P(None, 'row', 'col'), may hold values from -6 to 6
- inverses: float32 [4, 512, 512], replicated, may hold values from -0.5 to 2, as said below
Outputs:
- solved: float32 [4, 512, 128], P(None, 'col')
- remaining: float32 [6, 8, 32, 128, 128], P(None, 'row', 'col')
Inputs may be any that keep to these rules, and one draw needn't show every extreme that they name: `inverses`: each block is lower triangular with its diagonal between 0.5 and 2 and entries below it of magnitude at most 4 / sqrt(512).
All inputs are finite; a program needn't handle non-finite values.
Results may differ from a plain program's by a relative error of at most 0.00011.
Values sent between devices are 32-bit elements; how exact they have to be, the bound alone decides.
A program may use at most 64 MiB of HBM per device.

v0:
```python
import jax
import jax.numpy as jnp
from jax import lax
from jax.sharding import PartitionSpec as P


def shifted(block, axis, distance):
    devices = range(lax.axis_size(axis))
    route = [((i - distance) % len(devices), i) for i in devices]
    return lax.ppermute(block, axis, route)


def broadcast(x, axis, root):
    mine = lax.axis_index(axis) == root
    return lax.psum(jnp.where(mine, x, jnp.zeros_like(x)), axis)


def group_reduce(update, member, steps, groups):
    blocks = update.shape[0]
    nrhs = update.shape[2]
    split = update.reshape(blocks, steps, update.shape[1] // steps, nrhs)
    total = lax.dynamic_index_in_dim(split, member, 1, keepdims=False)
    for offset in range(1, steps):
        piece = lax.dynamic_index_in_dim(split, (member + offset) % steps, 1, keepdims=False)
        total = total + shifted(piece, "col", offset * groups)
    return total


def on_device(factor, rhs, inverses):
    steps = inverses.shape[0]
    blocks = factor.shape[0]
    width = factor.shape[3]
    quarter = rhs.shape[3]
    nrhs = rhs.shape[4]
    row_count = lax.axis_size("row")
    col_count = lax.axis_size("col")
    groups = col_count // steps
    row_pos = lax.axis_index("row")
    col_pos = lax.axis_index("col")
    member = col_pos // groups
    group = col_pos % groups
    block_ids = (jnp.arange(blocks, dtype=jnp.int32) * row_count + row_pos) * groups + group
    panel = factor[:, 0, 0]
    current = rhs[:, 0, 0]
    solved_list = []
    for k in range(steps):
        owner_row = k // groups
        owner_group = k % groups
        placed = lax.dynamic_update_slice(
            jnp.zeros((width, nrhs), jnp.float32),
            current[0],
            (member * quarter, jnp.zeros((), jnp.int32)),
        )
        contrib = placed
        is_owner = jnp.logical_and(row_pos == owner_row, group == owner_group)
        contrib = jnp.where(is_owner, contrib, jnp.zeros_like(contrib))
        complete = lax.psum(contrib, "col")
        solved_block = jnp.dot(inverses[k], complete, precision=lax.Precision.HIGHEST)
        solved_block = broadcast(solved_block, "row", owner_row)
        solved_list.append(solved_block)
        keep = (block_ids > k).astype(jnp.float32)[:, None, None]

        def column_update(solved_now=solved_block, keep_now=keep):
            return (
                jnp.einsum("rji,jh->rih", panel, solved_now, precision=lax.Precision.HIGHEST)
                * keep_now
            )

        def no_update():
            return jnp.zeros((blocks, width, nrhs), jnp.float32)

        update = lax.cond(member == k, column_update, no_update)
        current = current - group_reduce(update, member, steps, groups)
    stacked = jnp.stack(solved_list)
    share = width // col_count
    solved_rows = lax.dynamic_slice_in_dim(stacked, col_pos * share, share, 1)
    return (solved_rows, current[:, None, None])


def solution(mesh):
    in_specs = (P(None, "row", "col", None, None), P(None, "row", "col", None, None), P())
    out_specs = (P(None, "col", None), P(None, "row", "col", None, None))
    return jax.shard_map(
        on_device, mesh=mesh, in_specs=in_specs, out_specs=out_specs, check_vma=False
    )
```

profile of v0, /device:TPU:11, one launch (start us, length us, event | category | flops | bytes accessed | tf_op | source)
XLA Modules:
  0.0 976.8 jit_solution(4131290574086656395)
XLA Ops:
  7.2 0.0 all-reduce.9.cloned.1.call-start
  7.3 0.9 bitcast_dynamic-update-slice_fusion
  8.1 0.7 copy-done.5
  8.8 0.0 all-reduce.9.cloned.1.call-update
  8.9 0.0 all-reduce.11.cloned.1.call-start
  9.0 6.6 copy.5
  15.6 138.1 %all-reduce.9.cloned.1.call-done = f32[512,128]{1,0:T(8,128)} async-done(((f32[512,128]{1,0:T(8,128)}), f32[512,128]{1,0:T(8,128)}) %all-reduce.9.cloned.1.call-update) | async-done | bytes 262160 | tf_op jit(solution)/shard_map/psum | solution.py:57
  153.7 3.3 fusion.7
  156.9 0.0 all-reduce.11.cloned.1.call-update
  156.9 0.0 all-reduce.13.cloned.1.call-start
  157.0 63.1 %all-reduce.11.cloned.1.call-done = f32[512,128]{0,1:T(8,128)} async-done(((f32[512,128]{0,1:T(8,128)}), f32[512,128]{0,1:T(8,128)}) %all-reduce.11.cloned.1.call-update) | async-done | bytes 262160 | tf_op jit(solution)/shard_map/psum | solution.py:15
  220.1 0.2 conditional.4
  220.1 0.2 reshape.81
  220.3 0.9 dynamic-slice_bitcast_fusion.11
  221.1 1.2 collective-permute-start
  222.3 8.0 collective-permute-start.1
  230.3 5.2 collective-permute-done
  235.5 1.4 collective-permute-done.1
  236.8 11.6 %collective-permute-done.2 = f32[6,128,128]{2,1,0:T(8,128)} collective-permute-done((f32[6,128,128]{2,1,0:T(8,128)S(1)}, f32[6,128,128]{2,1,0:T(8,128)}, u32[]{:S(2)}, u32[]{:S(2)}) %collective-permute-start.2) | collective-permute-done | bytes 393248 | tf_op jit(solution)/shard_map/ppermute | solution.py:10
  248.4 1.1 fusion.28
  249.6 0.7 copy-done.6
  250.3 0.0 all-reduce.13.cloned.1.call-update
  250.3 0.0 all-reduce.15.cloned.1.call-start
  250.3 143.1 %all-reduce.13.cloned.1.call-done = f32[512,128]{1,0:T(8,128)} async-done(((f32[512,128]{1,0:T(8,128)}), f32[512,128]{1,0:T(8,128)}) %all-reduce.13.cloned.1.call-update) | async-done | bytes 262160 | tf_op jit(solution)/shard_map/psum | solution.py:57
  393.5 3.3 fusion.6
  396.7 0.0 all-reduce.17.cloned.1.call-start
  396.8 63.1 %all-reduce.15.cloned.1.call-done = f32[512,128]{0,1:T(8,128)} async-done(((f32[512,128]{0,1:T(8,128)}), f32[512,128]{0,1:T(8,128)}) %all-reduce.15.cloned.1.call-update) | async-done | bytes 262160 | tf_op jit(solution)/shard_map/psum | solution.py:15
  459.9 7.2 conditional.5
  459.9 7.2 convolution_multiply_fusion.1
  467.0 0.9 dynamic-slice_bitcast_fusion.8
  467.9 1.5 collective-permute-start.5
  469.3 6.5 collective-permute-done.3
  475.9 1.4 collective-permute-done.4
  477.3 11.0 %collective-permute-done.5 = f32[6,128,128]{2,1,0:T(8,128)} collective-permute-done((f32[6,128,128]{2,1,0:T(8,128)S(1)}, f32[6,128,128]{2,1,0:T(8,128)}, u32[]{:S(2)}, u32[]{:S(2)}) %collective-permute-start.5) | collective-permute-done | bytes 393248 | tf_op jit(solution)/shard_map/ppermute | solution.py:10
  488.2 1.1 fusion.25
  489.4 0.7 copy-done.7
  490.1 0.0 all-reduce.19.cloned.1.call-start
  490.2 142.5 %all-reduce.17.cloned.1.call-done = f32[512,128]{1,0:T(8,128)} async-done(((f32[512,128]{1,0:T(8,128)}), f32[512,128]{1,0:T(8,128)}) %all-reduce.17.cloned.1.call-update) | async-done | bytes 262160 | tf_op jit(solution)/shard_map/psum | solution.py:57
  632.7 3.3 fusion.5
  635.9 0.0 all-reduce.21.cloned.1.call-start
  636.0 63.1 %all-reduce.19.cloned.1.call-done = f32[512,128]{0,1:T(8,128)} async-done(((f32[512,128]{0,1:T(8,128)}), f32[512,128]{0,1:T(8,128)}) %all-reduce.19.cloned.1.call-update) | async-done | bytes 262160 | tf_op jit(solution)/shard_map/psum | solution.py:15
  699.1 0.2 conditional.6
  699.1 0.2 reshape.85
  699.2 0.9 dynamic-slice_bitcast_fusion.5
  700.1 8.2 collective-permute-start.6
  708.3 1.8 collective-permute-start.8
  710.1 14.3 %collective-permute-done.6 = f32[6,128,128]{2,1,0:T(8,128)S(1)} collective-permute-done((f32[6,128,128]{2,1,0:T(8,128)}, f32[6,128,128]{2,1,0:T(8,128)S(1)}, u32[]{:S(2)}, u32[]{:S(2)}) %collective-permute-start.6) | collective-permute-done | bytes 393248 | tf_op jit(solution)/shard_map/ppermute | solution.py:10
  724.4 1.9 collective-permute-done.8
  726.3 1.1 fusion.22
  727.5 0.7 copy-done.4
  728.2 0.0 all-reduce.23.cloned.1.call-start
  728.2 144.8 %all-reduce.21.cloned.1.call-done = f32[512,128]{1,0:T(8,128)} async-done(((f32[512,128]{1,0:T(8,128)}), f32[512,128]{1,0:T(8,128)}) %all-reduce.21.cloned.1.call-update) | async-done | bytes 262160 | tf_op jit(solution)/shard_map/psum | solution.py:57
  873.1 3.3 fusion.4
  876.4 63.1 %all-reduce.23.cloned.1.call-done = f32[512,128]{0,1:T(8,128)} async-done(((f32[512,128]{0,1:T(8,128)}), f32[512,128]{0,1:T(8,128)}) %all-reduce.23.cloned.1.call-update) | async-done | bytes 262160 | tf_op jit(solution)/shard_map/psum | solution.py:15
  939.5 0.2 conditional.7
  939.5 0.2 reshape.87
  939.7 1.1 dynamic-slice_bitcast_fusion.2
  940.7 8.8 collective-permute-start.10
  949.6 1.5 collective-permute-start.9
  951.0 0.1 fusion.31
  951.2 0.7 copy.10
  951.9 4.6 collective-permute-done.10
  956.5 11.4 %collective-permute-done.11 = f32[6,128,128]{2,1,0:T(8,128)} collective-permute-done((f32[6,128,128]{2,1,0:T(8,128)}, f32[6,128,128]{2,1,0:T(8,128)}, u32[]{:S(2)}, u32[]{:S(2)}) %collective-permute-start.11) | collective-permute-done | bytes 393248 | tf_op jit(solution)/shard_map/ppermute | solution.py:10
  967.9 2.1 fusion.19
  (35 shorter events, 0.3 us)
Async XLA Ops:
  7.2 146.5 %all-reduce.9.cloned.1.call-start = ((), (), s32[]{:S(2)}) async-start(), calls=%async_computation | async-start | bytes 524288 | tf_op jit(solution)/shard_map/psum | solution.py:57
  8.1 0.7 copy-start.5
  8.9 211.2 %all-reduce.11.cloned.1.call-start = ((), (), s32[]{:S(2)}) async-start(), calls=%async_computation.1 | async-start | bytes 524288 | tf_op jit(solution)/shard_map/psum | solution.py:15
  156.9 236.5 %all-reduce.13.cloned.1.call-start = ((), (), s32[]{:S(2)}) async-start(), calls=%async_computation.2 | async-start | bytes 524288 | tf_op jit(solution)/shard_map/psum | solution.py:57
  220.3 28.2 %copy-start.8 = (f32[6,1,1,128,128]{4,3,2,1,0:T(8,128)S(1)}, f32[6,1,1,128,128]{4,3,2,1,0:T(8,128)}, u32[]{:S(2)}) copy-start(f32[6,1,1,128,128]{4,3,2,1,0:T(8,128)} %param.12) | copy-start | bytes 1179652
  221.1 14.4 %collective-permute-start = (f32[6,128,128]{2,1,0:T(8,128)}, f32[6,128,128]{2,1,0:T(8,128)S(1)}, u32[]{:S(2)}, u32[]{:S(2)}) collective-permute-start(f32[6,128,128]{2,1,0:T(8,128)} %get-tuple-element.79), channel_id=1, source_target_pairs={{24,0},{25,1},{26,2},{27,3},{28,4},{29,5},{30,6},{31,7},{0,8},{1,9... | collective-permute-start | bytes 1179656 | tf_op jit(solution)/shard_map/ppermute | solution.py:10
  222.3 14.5 %collective-permute-start.1 = (f32[6,128,128]{2,1,0:T(8,128)S(1)}, f32[6,128,128]{2,1,0:T(8,128)S(1)}, u32[]{:S(2)}, u32[]{:S(2)}) collective-permute-start(f32[6,128,128]{2,1,0:T(8,128)S(1)} %get-tuple-element.81), channel_id=1, source_target_pairs={{16,0},{17,1},{18,2},{19,3},{20,4},{21,5},{22,6},{23,7},{24,8},{25... | collective-permute-start | bytes 1179656 | tf_op jit(solution)/shard_map/ppermute | solution.py:10
  230.3 18.1 %collective-permute-start.2 = (f32[6,128,128]{2,1,0:T(8,128)S(1)}, f32[6,128,128]{2,1,0:T(8,128)}, u32[]{:S(2)}, u32[]{:S(2)}) collective-permute-start(f32[6,128,128]{2,1,0:T(8,128)S(1)} %get-tuple-element.80), channel_id=1, source_target_pairs={{8,0},{9,1},{10,2},{11,3},{12,4},{13,5},{14,6},{15,7},{16,8},{17,9... | collective-permute-start | bytes 1179656 | tf_op jit(solution)/shard_map/ppermute | solution.py:10
  249.6 0.7 copy-start.6
  250.3 209.6 %all-reduce.15.cloned.1.call-start = ((), (), s32[]{:S(2)}) async-start(), calls=%async_computation.3 | async-start | bytes 524288 | tf_op jit(solution)/shard_map/psum | solution.py:15
  396.7 235.9 %all-reduce.17.cloned.1.call-start = ((), (), s32[]{:S(2)}) async-start(), calls=%async_computation.4 | async-start | bytes 524288 | tf_op jit(solution)/shard_map/psum | solution.py:57
  467.9 8.0 collective-permute-start.3
  467.9 9.4 collective-permute-start.4
  467.9 20.4 %collective-permute-start.5 = (f32[6,128,128]{2,1,0:T(8,128)S(1)}, f32[6,128,128]{2,1,0:T(8,128)}, u32[]{:S(2)}, u32[]{:S(2)}) collective-permute-start(f32[6,128,128]{2,1,0:T(8,128)S(1)} %get-tuple-element.77), channel_id=1, source_target_pairs={{8,0},{9,1},{10,2},{11,3},{12,4},{13,5},{14,6},{15,7},{16,8},{17,9... | collective-permute-start | bytes 1179656 | tf_op jit(solution)/shard_map/ppermute | solution.py:10
  489.4 0.7 copy-start.7
  490.1 208.9 %all-reduce.19.cloned.1.call-start = ((), (), s32[]{:S(2)}) async-start(), calls=%async_computation.5 | async-start | bytes 524288 | tf_op jit(solution)/shard_map/psum | solution.py:15
  635.9 237.1 %all-reduce.21.cloned.1.call-start = ((), (), s32[]{:S(2)}) async-start(), calls=%async_computation.6 | async-start | bytes 524288 | tf_op jit(solution)/shard_map/psum | solution.py:57
  700.1 24.3 %collective-permute-start.6 = (f32[6,128,128]{2,1,0:T(8,128)}, f32[6,128,128]{2,1,0:T(8,128)S(1)}, u32[]{:S(2)}, u32[]{:S(2)}) collective-permute-start(f32[6,128,128]{2,1,0:T(8,128)} %get-tuple-element.73), channel_id=1, source_target_pairs={{24,0},{25,1},{26,2},{27,3},{28,4},{29,5},{30,6},{31,7},{0,8},{1,9... | collective-permute-start | bytes 1179656 | tf_op jit(solution)/shard_map/ppermute | solution.py:10
  708.3 16.1 %collective-permute-start.7 = (f32[6,128,128]{2,1,0:T(8,128)S(1)}, f32[6,128,128]{2,1,0:T(8,128)S(1)}, u32[]{:S(2)}, u32[]{:S(2)}) collective-permute-start(f32[6,128,128]{2,1,0:T(8,128)S(1)} %get-tuple-element.75), channel_id=1, source_target_pairs={{16,0},{17,1},{18,2},{19,3},{20,4},{21,5},{22,6},{23,7},{24,8},{25... | collective-permute-start | bytes 1179656 | tf_op jit(solution)/shard_map/ppermute | solution.py:10
  708.3 18.0 %collective-permute-start.8 = (f32[6,128,128]{2,1,0:T(8,128)S(1)}, f32[6,128,128]{2,1,0:T(8,128)}, u32[]{:S(2)}, u32[]{:S(2)}) collective-permute-start(f32[6,128,128]{2,1,0:T(8,128)S(1)} %get-tuple-element.74), channel_id=1, source_target_pairs={{8,0},{9,1},{10,2},{11,3},{12,4},{13,5},{14,6},{15,7},{16,8},{17,9... | collective-permute-start | bytes 1179656 | tf_op jit(solution)/shard_map/ppermute | solution.py:10
  727.4 0.7 copy-start.4
  728.2 211.3 %all-reduce.23.cloned.1.call-start = ((), (), s32[]{:S(2)}) async-start(), calls=%async_computation.7 | async-start | bytes 524288 | tf_op jit(solution)/shard_map/psum | solution.py:15
  939.6 11.4 %copy-start = (f32[512,128]{0,1:T(8,128)S(1)}, f32[512,128]{0,1:T(8,128)}, u32[]{:S(2)}) copy-start(f32[512,128]{0,1:T(8,128)} %all-reduce.11.cloned.1.call-done) | copy-start | bytes 786436
  939.7 11.4 %copy-start.1 = (f32[512,128]{0,1:T(8,128)S(1)}, f32[512,128]{0,1:T(8,128)}, u32[]{:S(2)}) copy-start(f32[512,128]{0,1:T(8,128)} %all-reduce.15.cloned.1.call-done) | copy-start | bytes 786436
  939.7 11.4 %copy-start.2 = (f32[512,128]{0,1:T(8,128)S(1)}, f32[512,128]{0,1:T(8,128)}, u32[]{:S(2)}) copy-start(f32[512,128]{0,1:T(8,128)} %all-reduce.19.cloned.1.call-done) | copy-start | bytes 786436
  939.7 11.4 %copy-start.3 = (f32[512,128]{0,1:T(8,128)S(1)}, f32[512,128]{0,1:T(8,128)}, u32[]{:S(2)}) copy-start(f32[512,128]{0,1:T(8,128)} %all-reduce.23.cloned.1.call-done) | copy-start | bytes 786436
  940.7 15.8 %collective-permute-start.10 = (f32[6,128,128]{2,1,0:T(8,128)}, f32[6,128,128]{2,1,0:T(8,128)}, u32[]{:S(2)}, u32[]{:S(2)}) collective-permute-start(f32[6,128,128]{2,1,0:T(8,128)} %get-tuple-element.72), channel_id=1, source_target_pairs={{16,0},{17,1},{18,2},{19,3},{20,4},{21,5},{22,6},{23,7},{24,8},{25... | collective-permute-start | bytes 1179656 | tf_op jit(solution)/shard_map/ppermute | solution.py:10
  949.6 18.3 %collective-permute-start.11 = (f32[6,128,128]{2,1,0:T(8,128)}, f32[6,128,128]{2,1,0:T(8,128)}, u32[]{:S(2)}, u32[]{:S(2)}) collective-permute-start(f32[6,128,128]{2,1,0:T(8,128)} %get-tuple-element.71), channel_id=1, source_target_pairs={{8,0},{9,1},{10,2},{11,3},{12,4},{13,5},{14,6},{15,7},{16,8},{17,9... | collective-permute-start | bytes 1179656 | tf_op jit(solution)/shard_map/ppermute | solution.py:10
  949.6 18.3 %collective-permute-start.9 = (f32[6,128,128]{2,1,0:T(8,128)}, f32[6,128,128]{2,1,0:T(8,128)}, u32[]{:S(2)}, u32[]{:S(2)}) collective-permute-start(f32[6,128,128]{2,1,0:T(8,128)} %get-tuple-element.70), channel_id=1, source_target_pairs={{24,0},{25,1},{26,2},{27,3},{28,4},{29,5},{30,6},{31,7},{0,8},{1,9... | collective-permute-start | bytes 1179656 | tf_op jit(solution)/shard_map/ppermute | solution.py:10
Sparse Core Ops, SparseCore 0:
  12.0 141.5 all-reduce.8
  157.1 62.9 all-reduce.10
  250.4 142.9 all-reduce.12
  396.9 62.9 all-reduce.14
  490.2 142.3 all-reduce.16
  636.1 62.9 all-reduce.18
  728.3 144.7 all-reduce.20
  876.5 62.9 all-reduce.22
where the time goes:
time: 981 us; the launch traced here: 977 us
  waiting for transfers between devices  890 us (91%)
  starting transfers between devices  31.3 us (3%)
  matrix products  20.2 us (2%)
  between operations  14.4 us (1%)
  local copies, waits for them, and re-layouts  14.3 us (1%)
    psum x4, waiting for transfers between devices, on_device(): complete = lax.psum(contrib, 'col')  569 us
    psum x4, waiting for transfers between devices, broadcast(): return lax.psum(jnp.where(mine, x, jnp.zeros_like(x)), axis)  252 us
    ppermute x12, waiting for transfers between devices, shifted(): return lax.ppermute(block, axis, route)  69.2 us
    ppermute x12, starting transfers between devices, shifted(): return lax.ppermute(block, axis, route)  31 us
  transfers between devices with their start and end apart: 20, of which 18 were waited for; matrix products, arithmetic and copies ran while one was open for 1% of the time, Pallas kernels for 0%

commit v1 on v0

v1 whole, which is shorter than its diff:
```python
import functools

import jax
import jax.numpy as jnp
from jax import lax
from jax.experimental import pallas as pl
from jax.experimental.pallas import tpu as pltpu
from jax.sharding import PartitionSpec as P

MESH = pl.DeviceIdType.MESH
F32 = jnp.float32
BF16 = jnp.bfloat16


def split(x):
    hi = x.astype(BF16)
    return hi, (x - hi.astype(F32)).astype(BF16)


def product(x, hi, lo, transposed=False):
    dims = (((1,), (1 if transposed else 0,)), ((), ()))
    m = x.shape[0]
    x_hi, x_lo = split(x)
    both = lax.dot_general(
        jnp.concatenate([x_hi, x_lo], axis=0), hi, dims, preferred_element_type=F32
    )
    return both[:m] + (both[m:] + lax.dot_general(x_hi, lo, dims, preferred_element_type=F32))


def assemble(tiles):
    blocks = tiles.reshape(4, 64, 128)
    return jnp.concatenate([blocks[b] for b in range(4)], axis=1)


def kernel(
    factor, rhs, inverses, solved_out, remaining_out,
    f32_buf, f_hi, f_lo, inv_f32, inv_hi, inv_lo, rhs_buf,
    first, own, direct, u_in, u_out, tiles, gathered, parts, received, turned, solved_in,
    f_sem, inv_sem, rhs_sem, self_sem,
    first_send, first_recv, own_send, own_recv, direct_send, direct_recv, u_send, u_recv,
    scatter_send, scatter_recv, gather_send, gather_recv, pair_send, pair_recv,
    part_send, part_recv, solved_send, solved_recv,
):
    row = lax.axis_index("row")
    col = lax.axis_index("col")
    y = col // 8
    z = lax.rem(col, 8)
    core = lax.rem(row, 2)
    x = row // 2
    chip = x * 8 + z
    blocks = f_hi.shape[0]

    on_chain = (row == 0) & (y < z) & (z <= 3)
    starts = on_chain & (y == 0)
    solves = on_chain & (z == y + 1)
    source = solves | ((row == 0) & (y == 0) & (z == 3))
    gives_first = (row == 0) & (z == 0)
    gives_own = (row == 0) & (z >= 1) & (z <= 3)

    def remote(src, dst, send, recv, to_row, to_col):
        return pltpu.make_async_remote_copy(
            src_ref=src, dst_ref=dst, send_sem=send, recv_sem=recv,
            device_id=(to_row, to_col), device_id_type=MESH,
        )

    def landed(ref, sem):
        remote(ref, ref, sem, sem, row, col).wait_recv()

    def left(ref, sem):
        remote(ref, ref, sem, sem, row, col).wait_send()

    barrier = pltpu.get_barrier_semaphore()

    def greet(to_row, to_col):
        pl.semaphore_signal(barrier, inc=1, device_id=(to_row, to_col), device_id_type=MESH)

    for d in range(1, 4):
        greet(row, lax.rem(col + 8 * d, 32))

    @pl.when(starts)
    def _():
        for p in range(4):
            greet(0, p * 8)

    @pl.when(on_chain & (y > 0))
    def _():
        greet(0, (y - 1) * 8 + y)

    source_col = jnp.where(y == 0, 3, (y - 1) * 8 + y)

    @pl.when(jnp.logical_not((row == 0) & (col == source_col)))
    def _():
        greet(0, source_col)

    def f_load(a):
        return pltpu.make_async_copy(factor.at[a, 0, 0], f32_buf.at[a], f_sem.at[a])

    def inv_load(k, slot):
        return pltpu.make_async_copy(inverses.at[k], inv_f32.at[slot], inv_sem.at[slot])

    @pl.when(starts)
    def _():
        inv_load(0, 0).start()

    @pl.when(solves)
    def _():
        inv_load(z, 1).start()

    for a in range(blocks):
        f_load(a).start()
    rhs_load = pltpu.make_async_copy(rhs.at[:, 0, 0], rhs_buf, rhs_sem)
    rhs_load.start()
    self_load = pltpu.make_async_copy(rhs.at[0, 0, 0], own.at[y], self_sem)

    @pl.when(solves)
    def _():
        self_load.start()

    def split_inverse(k, slot):
        inv_load(k, slot).wait()
        hi, lo = split(inv_f32[slot])
        inv_hi[slot] = hi
        inv_lo[slot] = lo

    def split_factor(a):
        f_load(a).wait()
        hi, lo = split(f32_buf[a])
        f_hi[a] = hi
        f_lo[a] = lo

    @pl.when(starts)
    def _():
        split_inverse(0, 0)

    @pl.when(solves)
    def _():
        split_inverse(z, 1)

    split_factor(0)

    greeted = 3
    greeted += jnp.where(gives_first, 3, 0)
    greeted += jnp.where(source, jnp.where((y == 0) & (z == 3), 63, 64), 0)
    greeted += jnp.where(solves & (z < 3), 3 - z, 0)
    pl.semaphore_wait(barrier, greeted)

    @pl.when(gives_first)
    def _():
        for t in range(1, 4):
            remote(rhs.at[0, 0, 0], first.at[y], first_send, first_recv.at[y], 0, t).start()

    @pl.when(gives_own & (y != z - 1))
    def _():
        remote(rhs.at[0, 0, 0], own.at[y], own_send, own_recv.at[y], 0, (z - 1) * 8 + z).start()

    def split_rest():
        lax.fori_loop(1, blocks, lambda a, _: (split_factor(a), 0)[1], 0)

    @pl.when(jnp.logical_not(starts))
    def _():
        split_rest()

    def store_tiles(s):
        for c in range(2):
            for b in range(4):
                tiles[c, b * 8 : (b + 1) * 8] = s[
                    64 * c : 64 * (c + 1), 128 * b : 128 * (b + 1)
                ].reshape(8, 8, 128)

    def scatter(plane):
        def send(i, _):
            to_row = i // 8
            to_z = lax.rem(i, 8)
            here = (to_row == row) & (plane * 8 + to_z == col)
            piece = (lax.rem(to_row, 2), (to_row // 2) * 8 + to_z)

            @pl.when(jnp.logical_not(here))
            def _():
                remote(
                    tiles.at[piece], gathered.at[piece], scatter_send, scatter_recv,
                    to_row, plane * 8 + to_z,
                ).start()

            return 0

        lax.fori_loop(0, 64, send, 0)

    @pl.when(on_chain)
    def _():
        @pl.when(y == 0)
        def _():
            for p in range(4):
                landed(first.at[p], first_recv.at[p])
            v = jnp.concatenate([first[p].T for p in range(4)], axis=1)
            s = product(v, inv_hi[0], inv_lo[0], True)
            direct_value = s
            for c in range(2):
                for b in range(4):
                    direct[c, b * 8 : (b + 1) * 8] = direct_value[
                        64 * c : 64 * (c + 1), 128 * b : 128 * (b + 1)
                    ].reshape(8, 8, 128)

        @pl.when(y > 0)
        def _():
            landed(direct, direct_recv)

        s = jnp.concatenate([assemble(direct[0]), assemble(direct[1])], axis=0)
        u_out[...] = product(s, f_hi[0], f_lo[0])

        @pl.when(z > y + 1)
        def _():
            remote(u_out, u_in.at[y], u_send, u_recv.at[y], 0, (z - 1) * 8 + z).start()

        @pl.when((y == 0) & (z == 3))
        def _():
            tiles[...] = direct[...]
            gathered[core, chip] = direct[core, chip]
            scatter(0)

        @pl.when(z == y + 1)
        def _():
            self_load.wait()
            for p in range(4):

                @pl.when(p != y)
                def _(p=p):
                    landed(own.at[p], own_recv.at[p])

            for j in range(2):

                @pl.when(j < y)
                def _(j=j):
                    landed(u_in.at[j], u_recv.at[j])
                    u_out[...] += u_in[j]

            v = jnp.concatenate([own[p].T for p in range(4)], axis=1) - u_out[...]
            store_tiles(product(v, inv_hi[1], inv_lo[1], True))
            for t in range(2, 4):

                @pl.when(t > z)
                def _(t=t):
                    remote(tiles, direct, direct_send.at[t - 2], direct_recv, 0, z * 8 + t).start()

            scatter(z)

        @pl.when(y == 0)
        def _():
            split_rest()

    @pl.when(jnp.logical_not((row == 0) & (col == 3)))
    def _():
        landed(gathered.at[core, chip], scatter_recv)

    mine = gathered.at[core, chip]

    def send_tile(i, _):
        to_row = lax.rem(x + i // 8, 4) * 2 + core
        to_col = y * 8 + lax.rem(z + lax.rem(i, 8), 8)
        remote(mine, mine, gather_send, gather_recv, to_row, to_col).start()
        return 0

    lax.fori_loop(1, 32, send_tile, 0)
    landed(gathered.at[core, pl.ds(0, 31)], gather_recv)
    other = row + 1 - 2 * core
    pair = remote(gathered.at[core], gathered.at[core], pair_send, pair_recv, other, col)
    pair.start()

    keep = jnp.where((row == 0) & (z <= y), 0.0, 1.0).astype(F32)

    def update(half):
        s = assemble(gathered[half])

        def one(a, _):
            u = product(s, f_hi[a], f_lo[a])
            u = jnp.where(a == 0, u * keep, u)
            for p in range(4):
                parts[p, half, a] = u[:, 128 * p : 128 * (p + 1)]

            received[y, half, a] = parts[y, half, a]
            for d in range(1, 4):
                to = lax.rem(y + d, 4)
                remote(
                    parts.at[to, half, a], received.at[y, half, a], part_send, part_recv.at[y, half],
                    row, to * 8 + z,
                ).start()
            return 0

        lax.fori_loop(0, blocks, one, 0)

    update(core)
    landed(gathered.at[1 - core], pair_recv)
    update(1 - core)

    for b in range(4):
        t = jnp.concatenate(
            [gathered[0, b * 8 : (b + 1) * 8], gathered[1, b * 8 : (b + 1) * 8]], axis=0
        ).reshape(128, 128)
        turned[b] = t.T
    rows = pl.ds(pl.multiple_of(z * 16, 16), 16)
    for d in range(1, 4):
        to = lax.rem(y + d, 4)
        remote(
            turned.at[to, rows], solved_in.at[y], solved_send, solved_recv.at[y], row, to * 8 + z
        ).start()
    solved_in[y] = turned[y, rows]

    rhs_load.wait()

    def reduce(k):
        def one(a, _):
            part = jnp.concatenate([received[k, 0, a], received[k, 1, a]], axis=0)
            rhs_buf[a] = rhs_buf[a] - part.T
            return 0

        lax.fori_loop(0, blocks, one, 0)

    for k in range(4):

        @pl.when(k != y)
        def _(k=k):
            landed(received.at[k, 0], part_recv.at[k, 0])
            landed(received.at[k, 1], part_recv.at[k, 1])

        reduce(k)
    remaining_out[...] = rhs_buf[...]
    for k in range(4):

        @pl.when(k != y)
        def _(k=k):
            landed(solved_in.at[k], solved_recv.at[k])

    solved_out[...] = solved_in[...]

    left(solved_in.at[pl.ds(0, 3)], solved_send)
    left(received.at[pl.ds(0, 3)], part_send)
    pair.wait_send()
    left(gathered.at[core, pl.ds(0, 31)], gather_send)

    @pl.when(gives_first)
    def _():
        left(first.at[pl.ds(0, 3)], first_send)

    @pl.when(gives_own & (y != z - 1))
    def _():
        left(own.at[0], own_send)

    @pl.when(on_chain & (z > y + 1))
    def _():
        left(u_out, u_send)

    @pl.when(solves)
    def _():
        for t in range(2, 4):

            @pl.when(t > z)
            def _(t=t):
                left(tiles, direct_send.at[t - 2])

        left(tiles, scatter_send)

    @pl.when((row == 0) & (col == 3))
    def _():
        left(tiles.at[0], scatter_send)
        left(tiles.at[1, pl.ds(0, 31)], scatter_send)


def solution(mesh):
    def on_device(factor, rhs, inverses):
        steps = inverses.shape[0]
        blocks, width, nrhs = factor.shape[0], factor.shape[3], rhs.shape[4]
        vmem, dma = pltpu.VMEM, pltpu.SemaphoreType.DMA
        solved, remaining = pl.pallas_call(
            kernel,
            out_shape=(
                jax.ShapeDtypeStruct((steps, 16, nrhs), F32),
                jax.ShapeDtypeStruct((blocks, 128, nrhs), F32),
            ),
            in_specs=[pl.BlockSpec(memory_space=pl.ANY)] * 3,
            out_specs=(
                pl.BlockSpec(memory_space=pltpu.VMEM),
                pl.BlockSpec(memory_space=pltpu.VMEM),
            ),
            scratch_shapes=[
                vmem((blocks, width, width), F32),
                vmem((blocks, width, width), BF16),
                vmem((blocks, width, width), BF16),
                vmem((2, width, width), F32),
                vmem((2, width, width), BF16),
                vmem((2, width, width), BF16),
                vmem((blocks, 128, nrhs), F32),
                vmem((4, 128, nrhs), F32),
                vmem((4, 128, nrhs), F32),
                vmem((2, 32, 8, 128), F32),
                vmem((2, nrhs, width), F32),
                vmem((nrhs, width), F32),
                vmem((2, 32, 8, 128), F32),
                vmem((2, 32, 8, 128), F32),
                vmem((4, 2, blocks, 64, 128), F32),
                vmem((4, 2, blocks, 64, 128), F32),
                vmem((4, 128, nrhs), F32),
                vmem((4, 16, nrhs), F32),
                dma((blocks,)),
                dma((2,)),
                dma,
                dma,
                dma,
                dma((4,)),
                dma,
                dma((4,)),
                dma((2,)),
                dma,
                dma,
                dma((2,)),
                dma,
                dma,
                dma,
                dma,
                dma,
                dma,
                dma,
                dma((4, 2)),
                dma,
                dma((4,)),
            ],
            compiler_params=pltpu.CompilerParams(
                collective_id=0, has_side_effects=True, vmem_limit_bytes=56 * 2**20
            ),
        )(factor, rhs, inverses)
        return solved, remaining[:, None, None]

    return jax.shard_map(
        on_device,
        mesh=mesh,
        in_specs=(P(None, "row", "col", None, None), P(None, "row", "col", None, None), P()),
        out_specs=(P(None, "col", None), P(None, "row", "col", None, None)),
        check_vma=False,
    )
```

time: 981 us -> 68.6 us (0.07)
  the two profiles are of different devices: /device:TPU:11 before, /device:TPU:8 now
where the time goes in v1:
time: 68.6 us; the launch traced here: 68.5 us
  Pallas kernels  64.7 us (94%)
  local copies, waits for them, and re-layouts  3.14 us (5%)
    pallas_call x1, Pallas kernels, on_device(): pl.pallas_call(kernel, out_shape=(jax.ShapeDtypeStruct((steps, 16, nrhs),...  64.7 us
    unnamed x2, local copies, waits for them, and re-layouts  3.14 us

profile of v1, /device:TPU:8, one launch (start us, length us, event | category | flops | bytes accessed | tf_op | source)
XLA Modules:
  0.0 68.5 jit_solution(1889872458554670360)
XLA Ops:
  0.6 64.7 %shard_map.50 = (f32[4,16,128]{2,1,0:T(8,128)}, f32[6,128,128]{2,1,0:T(8,128)}) custom-call(f32[6,1,1,512,512]{4,3,2,1,0:T(8,128)} %factor.1, f32[6,1,1,128,128]{4,3,2,1,0:T(8,128)} %rhs.1, f32[4,512,512]{2,1,0:T(8,128)} %inverses.1), custom_call_target="tpu_custom_call" | custom-call | tf_op jit(solution)/shard_map/pallas_call | solution.py:372
  65.3 1.4 %copy.8 = f32[4,16,128]{2,1,0:T(8,128)} copy(f32[4,16,128]{2,1,0:T(8,128)} %get-tuple-element.10) | data formatting | bytes 65536
  66.7 1.8 %copy.9 = f32[6,1,1,128,128]{4,3,2,1,0:T(8,128)} copy(f32[6,1,1,128,128]{4,3,2,1,0:T(8,128)} %bitcast.3) | data formatting | bytes 786432

commit v2 on v1

v2 whole, which is shorter than its diff:
```python
import jax
import jax.numpy as jnp
from jax import lax
from jax.experimental import pallas as pl
from jax.experimental.pallas import tpu as pltpu
from jax.sharding import PartitionSpec as P

MESH = pl.DeviceIdType.MESH
F32 = jnp.float32
BF16 = jnp.bfloat16


def split(x):
    hi = x.astype(BF16)
    return hi, (x - hi.astype(F32)).astype(BF16)


def product(x, hi, lo, transposed=False):
    dims = (((1,), (1 if transposed else 0,)), ((), ()))
    m = x.shape[0]
    x_hi, x_lo = split(x)
    both = lax.dot_general(
        jnp.concatenate([x_hi, x_lo], axis=0), hi, dims, preferred_element_type=F32
    )
    return both[:m] + (both[m:] + lax.dot_general(x_hi, lo, dims, preferred_element_type=F32))


def kernel(
    factor, rhs, inverses, solved_out, remaining_out,
    f32_buf, f_hi, f_lo, inv_f32, inv_hi, inv_lo, rhs_buf, total,
    first, own, first_t, own_t, direct, u_in, u_out, s_out, gathered,
    parts, received, turned, solved_in,
    f_sem, inv_sem, rhs_sem, self_sem,
    first_send, first_recv, own_send, own_recv, direct_send, direct_recv, u_send, u_recv,
    plane_send, relay_send, plane_recv, part_send, part_recv, solved_send, solved_recv,
):
    row = lax.axis_index("row")
    col = lax.axis_index("col")
    y = col // 8
    z = lax.rem(col, 8)
    blocks = f_hi.shape[0]
    chunks, high = gathered.shape[0], gathered.shape[1]

    on_chain = (row == 0) & (y < z) & (z <= 3)
    starts = on_chain & (y == 0)
    solves = on_chain & (z == y + 1)
    opens = (row == 4) & (col == 0)
    gives_first = (row == 0) & (z == 0)
    gives_own = (row == 0) & (z >= 1) & (z <= 3)
    relay_row = jnp.where(y == 0, 4, 0)
    relays = row == relay_row

    def remote(src, dst, send, recv, to_row, to_col):
        return pltpu.make_async_remote_copy(
            src_ref=src, dst_ref=dst, send_sem=send, recv_sem=recv,
            device_id=(to_row, to_col), device_id_type=MESH,
        )

    def landed(ref, sem):
        remote(ref, ref, sem, sem, row, col).wait_recv()

    def left(ref, sem):
        remote(ref, ref, sem, sem, row, col).wait_send()

    def each(n, body):
        lax.fori_loop(0, n, lambda i, _: (body(i), 0)[1], 0)

    barrier = pltpu.get_barrier_semaphore()

    def greet(to_row, to_col):
        pl.semaphore_signal(barrier, inc=1, device_id=(to_row, to_col), device_id_type=MESH)

    @pl.when(starts | opens)
    def _():
        for p in range(4):
            greet(0, p * 8)

    for d in range(1, 4):
        greet(row, lax.rem(col + 8 * d, 32))

    @pl.when(relays & jnp.logical_not(opens))
    def _():
        greet(relay_row, jnp.where(y == 0, 0, (y - 1) * 8 + y))

    @pl.when(jnp.logical_not(relays))
    def _():
        greet(relay_row, col)

    def f_load(a):
        return pltpu.make_async_copy(factor.at[a, 0, 0], f32_buf.at[a], f_sem.at[a])

    def inv_load(k, slot):
        return pltpu.make_async_copy(inverses.at[k], inv_f32.at[slot], inv_sem.at[slot])

    @pl.when(starts | opens)
    def _():
        inv_load(0, 0).start()

    @pl.when(solves)
    def _():
        inv_load(z, 1).start()

    for a in range(blocks):
        f_load(a).start()
    rhs_load = pltpu.make_async_copy(rhs.at[:, 0, 0], rhs_buf, rhs_sem)
    rhs_load.start()
    self_load = pltpu.make_async_copy(rhs.at[0, 0, 0], own.at[y], self_sem)

    @pl.when(solves)
    def _():
        self_load.start()

    def split_inverse(k, slot):
        inv_load(k, slot).wait()
        hi, lo = split(inv_f32[slot])
        inv_hi[slot] = hi
        inv_lo[slot] = lo

    def split_factor(a):
        f_load(a).wait()
        hi, lo = split(f32_buf[a])
        f_hi[a] = hi
        f_lo[a] = lo

    @pl.when(starts | opens)
    def _():
        split_inverse(0, 0)

    @pl.when(solves)
    def _():
        split_inverse(z, 1)

    split_factor(0)

    greeted = 3
    greeted += jnp.where(gives_first, 4, 0)
    greeted += jnp.where(solves, 8, 0)
    greeted += jnp.where(opens, 7, 0)
    greeted += jnp.where(relays, 7, 0)
    pl.semaphore_wait(barrier, greeted)

    @pl.when(gives_first)
    def _():
        for t in range(1, 4):
            remote(rhs.at[0, 0, 0], first.at[y], first_send, first_recv.at[y], 0, t).start()
        remote(rhs.at[0, 0, 0], first.at[y], first_send, first_recv.at[y], 4, 0).start()

    @pl.when(gives_own & (y != z - 1))
    def _():
        remote(rhs.at[0, 0, 0], own.at[y], own_send, own_recv.at[y], 0, (z - 1) * 8 + z).start()

    def prepare():
        lax.fori_loop(1, blocks, lambda a, _: (split_factor(a), 0)[1], 0)
        rhs_load.wait()

        def turn(a):
            total[a] = rhs_buf[a].T

        each(blocks, turn)

    early = starts | opens

    @pl.when(jnp.logical_not(early))
    def _():
        prepare()

    def rows_of(q):
        return pl.ds(pl.multiple_of(q * high, high), high)

    def spread(q, plane):
        for t in range(8):
            remote(
                s_out.at[q], gathered.at[q], plane_send, plane_recv.at[q], 0, plane * 8 + t
            ).start()

    @pl.when(early)
    def _():
        for p in range(4):
            landed(first.at[p], first_recv.at[p])
            first_t[:, 128 * p : 128 * (p + 1)] = first[p].T

    @pl.when(opens)
    def _():
        def open_chunk(q):
            gathered[q] = product(first_t[rows_of(q)], inv_hi[0], inv_lo[0], True)
            for t in range(1, 8):
                remote(
                    gathered.at[q], gathered.at[q], plane_send, plane_recv.at[q], 4, t
                ).start()

        each(chunks, open_chunk)

    @pl.when(on_chain)
    def _():
        @pl.when(z == y + 1)
        def _():
            self_load.wait()
            for p in range(4):

                @pl.when(p != y)
                def _(p=p):
                    landed(own.at[p], own_recv.at[p])

                own_t[:, 128 * p : 128 * (p + 1)] = own[p].T

        def chain_chunk(q):
            @pl.when(y == 0)
            def _():
                direct[q] = product(first_t[rows_of(q)], inv_hi[0], inv_lo[0], True)

            @pl.when(y > 0)
            def _():
                landed(direct.at[q], direct_recv.at[q])

            u = product(direct[q], f_hi[0], f_lo[0])

            @pl.when(z > y + 1)
            def _():
                u_out[q] = u
                remote(
                    u_out.at[q], u_in.at[y, q], u_send, u_recv.at[y, q], 0, (z - 1) * 8 + z
                ).start()

            @pl.when(z == y + 1)
            def _():
                u_out[q] = own_t[rows_of(q)] - u
                for j in range(2):

                    @pl.when(j < y)
                    def _(j=j):
                        landed(u_in.at[j, q], u_recv.at[j, q])
                        u_out[q] = u_out[q] - u_in[j, q]

                s_out[q] = product(u_out[q], inv_hi[1], inv_lo[1], True)
                for t in range(2, 4):

                    @pl.when(t > z)
                    def _(t=t):
                        remote(
                            s_out.at[q], direct.at[q], direct_send, direct_recv.at[q], 0, z * 8 + t
                        ).start()

                @pl.when(z == 3)
                def _():
                    spread(q, 3)

        each(chunks, chain_chunk)

        @pl.when((z == y + 1) & (z < 3))
        def _():
            each(chunks, lambda q: spread(q, z))

    @pl.when(early)
    def _():
        prepare()

    keep = jnp.where((row == 0) & (z <= y), 0.0, 1.0).astype(F32)

    def plane_chunk(q):
        @pl.when(jnp.logical_not(opens))
        def _():
            landed(gathered.at[q], plane_recv.at[q])

        @pl.when(relays)
        def _():
            for t in range(1, 8):
                remote(
                    gathered.at[q], gathered.at[q], relay_send, plane_recv.at[q],
                    lax.rem(row + t, 8), col,
                ).start()

        s = gathered[q]

        def one(a):
            u = product(s, f_hi[a], f_lo[a])
            u = jnp.where(a == 0, u * keep, u)
            for p in range(4):
                parts[p, q, a] = u[:, 128 * p : 128 * (p + 1)]

            received[y, q, a] = parts[y, q, a]
            for d in range(1, 4):
                to = lax.rem(y + d, 4)
                remote(
                    parts.at[to, q, a], received.at[y, q, a], part_send, part_recv.at[y, q],
                    row, to * 8 + z,
                ).start()

        each(blocks, one)

    each(chunks, plane_chunk)

    for b in range(4):
        t = jnp.concatenate(
            [gathered[q, :, 128 * b : 128 * (b + 1)] for q in range(chunks)], axis=0
        )
        turned[b] = t.T
    rows = pl.ds(pl.multiple_of(z * 16, 16), 16)
    for d in range(1, 4):
        to = lax.rem(y + d, 4)
        remote(
            turned.at[to, rows], solved_in.at[y], solved_send, solved_recv.at[y], row, to * 8 + z
        ).start()
    solved_in[y] = turned[y, rows]

    for k in range(4):

        def reduce(q, k=k):
            @pl.when(k != y)
            def _():
                landed(received.at[k, q], part_recv.at[k, q])

            def one(a):
                total[a, rows_of(q)] = total[a, rows_of(q)] - received[k, q, a]

            each(blocks, one)

        each(chunks, reduce)

    for a in range(blocks):
        remaining_out[a] = total[a].T
    for k in range(4):

        @pl.when(k != y)
        def _(k=k):
            landed(solved_in.at[k], solved_recv.at[k])

    solved_out[...] = solved_in[...]

    left(solved_in.at[pl.ds(0, 3)], solved_send)
    left(received.at[pl.ds(0, 3)], part_send)

    @pl.when(relays)
    def _():
        for t in range(1, 8):
            left(gathered, relay_send)

    @pl.when(gives_first)
    def _():
        left(first, first_send)

    @pl.when(gives_own & (y != z - 1))
    def _():
        left(own.at[0], own_send)

    @pl.when(on_chain & (z > y + 1))
    def _():
        left(u_out, u_send)

    @pl.when(solves)
    def _():
        for t in range(2, 4):

            @pl.when(t > z)
            def _(t=t):
                left(s_out, direct_send)

        for t in range(8):
            left(s_out, plane_send)

    @pl.when(opens)
    def _():
        for t in range(1, 8):
            left(gathered, plane_send)


def write(solved, remaining, solved_out, remaining_out, sems):
    copies = [
        pltpu.make_async_copy(remaining, remaining_out, sems.at[0]),
        pltpu.make_async_copy(solved, solved_out, sems.at[1]),
    ]
    for c in copies:
        c.start()
    for c in copies:
        c.wait()


def solution(mesh):
    def on_device(factor, rhs, inverses):
        steps = inverses.shape[0]
        blocks, width, nrhs = factor.shape[0], factor.shape[3], rhs.shape[4]
        chunks = 4
        high = nrhs // chunks
        vmem, dma = pltpu.VMEM, pltpu.SemaphoreType.DMA
        shapes = (
            jax.ShapeDtypeStruct((steps, 16, nrhs), F32),
            jax.ShapeDtypeStruct((blocks, 128, nrhs), F32),
        )
        results = pl.pallas_call(
            kernel,
            out_shape=shapes,
            in_specs=[pl.BlockSpec(memory_space=pl.ANY)] * 3,
            out_specs=(pl.BlockSpec(memory_space=pltpu.VMEM),) * 2,
            scratch_shapes=[
                vmem((blocks, width, width), F32),
                vmem((blocks, width, width), BF16),
                vmem((blocks, width, width), BF16),
                vmem((2, width, width), F32),
                vmem((2, width, width), BF16),
                vmem((2, width, width), BF16),
                vmem((blocks, 128, nrhs), F32),
                vmem((blocks, nrhs, 128), F32),
                vmem((4, 128, nrhs), F32),
                vmem((4, 128, nrhs), F32),
                vmem((nrhs, width), F32),
                vmem((nrhs, width), F32),
                vmem((chunks, high, width), F32),
                vmem((2, chunks, high, width), F32),
                vmem((chunks, high, width), F32),
                vmem((chunks, high, width), F32),
                vmem((chunks, high, width), F32),
                vmem((4, chunks, blocks, high, 128), F32),
                vmem((4, chunks, blocks, high, 128), F32),
                vmem((4, 128, nrhs), F32),
                vmem((4, 16, nrhs), F32),
                dma((blocks,)),
                dma((2,)),
                dma,
                dma,
                dma,
                dma((4,)),
                dma,
                dma((4,)),
                dma,
                dma((chunks,)),
                dma,
                dma((2, chunks)),
                dma,
                dma,
                dma((chunks,)),
                dma,
                dma((4, chunks)),
                dma,
                dma((4,)),
            ],
            compiler_params=pltpu.CompilerParams(
                collective_id=0, has_side_effects=True, vmem_limit_bytes=56 * 2**20
            ),
        )(factor, rhs, inverses)
        solved, remaining = pl.pallas_call(
            write,
            out_shape=shapes,
            in_specs=[pl.BlockSpec(memory_space=pl.ANY)] * 2,
            out_specs=(pl.BlockSpec(memory_space=pl.ANY),) * 2,
            scratch_shapes=[dma((2,))],
        )(*results)
        return solved, remaining[:, None, None]

    return jax.shard_map(
        on_device,
        mesh=mesh,
        in_specs=(P(None, "row", "col", None, None), P(None, "row", "col", None, None), P()),
        out_specs=(P(None, "col", None), P(None, "row", "col", None, None)),
        check_vma=False,
    )
```

time: 68.6 us -> 70 us (1.020)
  the two profiles are of different devices: /device:TPU:8 before, /device:TPU:101 now
where the time goes in v2:
time: 70 us; the launch traced here: 69.9 us
  Pallas kernels  69.3 us (99%)
    pallas_call x1, Pallas kernels, on_device(): pl.pallas_call(kernel, out_shape=shapes, in_specs=[pl.BlockSpec(memory_sp...  55.3 us
    pallas_call x1, Pallas kernels, on_device(): pl.pallas_call(write, out_shape=shapes, in_specs=[pl.BlockSpec(memory_spa...  14 us

profile of v2, /device:TPU:101, one launch (start us, length us, event | category | flops | bytes accessed | tf_op | source)
XLA Modules:
  0.0 69.9 jit_solution(18378295194127889568)
XLA Ops:
  0.6 55.3 %shard_map.50 = (f32[4,16,128]{2,1,0:T(8,128)}, f32[6,128,128]{2,1,0:T(8,128)}) custom-call(f32[6,1,1,512,512]{4,3,2,1,0:T(8,128)} %factor.1, f32[6,1,1,128,128]{4,3,2,1,0:T(8,128)} %rhs.1, f32[4,512,512]{2,1,0:T(8,128)} %inverses.1), custom_call_target="tpu_custom_call" | custom-call | tf_op jit(solution)/shard_map/pallas_call | solution.py:388
  55.9 14.0 %shard_map.51 = (f32[4,16,128]{2,1,0:T(8,128)}, f32[6,128,128]{2,1,0:T(8,128)}) custom-call(f32[4,16,128]{2,1,0:T(8,128)} %get-tuple-element.6.solved, f32[6,128,128]{2,1,0:T(8,128)} %get-tuple-element.7.remaining), custom_call_target="tpu_custom_call" | custom-call | tf_op jit(solution)/shard_map/pallas_call | solution.py:439

commit v3 on v2

--- a/solution.py
+++ b/solution.py
@@ -8,6 +8,8 @@
 MESH = pl.DeviceIdType.MESH
 F32 = jnp.float32
 BF16 = jnp.bfloat16
+SIZES = (24, 24, 24, 24, 16, 16)
+CHUNKS = tuple((sum(SIZES[:q]), n) for q, n in enumerate(SIZES))
 
 
 def split(x):
@@ -27,7 +29,7 @@
 
 def kernel(
     factor, rhs, inverses, solved_out, remaining_out,
-    f32_buf, f_hi, f_lo, inv_f32, inv_hi, inv_lo, rhs_buf, total,
+    f32_buf, f_hi, f_lo, inv_f32, inv_hi, inv_lo, m_f32, m_hi, m_lo, rhs_buf, total,
     first, own, first_t, own_t, direct, u_in, u_out, s_out, gathered,
     parts, received, turned, solved_in,
     f_sem, inv_sem, rhs_sem, self_sem,
@@ -39,7 +41,6 @@
     y = col // 8
     z = lax.rem(col, 8)
     blocks = f_hi.shape[0]
-    chunks, high = gathered.shape[0], gathered.shape[1]
 
     on_chain = (row == 0) & (y < z) & (z <= 3)
     starts = on_chain & (y == 0)
@@ -47,7 +48,7 @@
     opens = (row == 4) & (col == 0)
     gives_first = (row == 0) & (z == 0)
     gives_own = (row == 0) & (z >= 1) & (z <= 3)
-    relay_row = jnp.where(y == 0, 4, 0)
+    relay_row = jnp.where(y == 0, 5, 1)
     relays = row == relay_row
 
     def remote(src, dst, send, recv, to_row, to_col):
@@ -78,9 +79,13 @@
     for d in range(1, 4):
         greet(row, lax.rem(col + 8 * d, 32))
 
-    @pl.when(relays & jnp.logical_not(opens))
-    def _():
-        greet(relay_row, jnp.where(y == 0, 0, (y - 1) * 8 + y))
+    @pl.when(relays)
+    def _():
+        greet(jnp.where(y == 0, 4, 0), jnp.where(y == 0, 0, (y - 1) * 8 + y))
+
+    @pl.when(on_chain & (y > 0))
+    def _():
+        greet(0, (y - 1) * 8 + y)
 
     @pl.when(jnp.logical_not(relays))
     def _():
@@ -96,7 +101,7 @@
     def _():
         inv_load(0, 0).start()
 
-    @pl.when(solves)
+    @pl.when(on_chain)
     def _():
         inv_load(z, 1).start()
 
@@ -126,16 +131,40 @@
     def _():
         split_inverse(0, 0)
 
-    @pl.when(solves)
+    split_factor(0)
+
+    def fold(source):
+        def some(b):
+            rows = pl.ds(pl.multiple_of(b * 128, 128), 128)
+            m_f32[rows] = source(rows)
+
+        each(4, some)
+
+    def split_m():
+        hi, lo = split(m_f32[...])
+        m_hi[...] = hi
+        m_lo[...] = lo
+
+    @pl.when(on_chain)
     def _():
         split_inverse(z, 1)
-
-    split_factor(0)
+        fold(lambda rows: product(f32_buf[0, rows], inv_hi[1], inv_lo[1], True))
+        split_m()
+
+        @pl.when(y == 0)
+        def _():
+            for b in range(4):
+                for c in range(4):
+                    f32_buf[0, 128 * b : 128 * (b + 1), 128 * c : 128 * (c + 1)] = inv_f32[
+                        0, 128 * c : 128 * (c + 1), 128 * b : 128 * (b + 1)
+                    ].T
+            fold(lambda rows: product(f32_buf[0, rows], m_hi[...], m_lo[...]))
+            split_m()
 
     greeted = 3
     greeted += jnp.where(gives_first, 4, 0)
-    greeted += jnp.where(solves, 8, 0)
-    greeted += jnp.where(opens, 7, 0)
+    greeted += jnp.where(solves | opens, 8, 0)
+    greeted += jnp.where(solves & (z < 3), 3 - z, 0)
     greeted += jnp.where(relays, 7, 0)
     pl.semaphore_wait(barrier, greeted)
 
@@ -165,90 +194,97 @@
         prepare()
 
     def rows_of(q):
-        return pl.ds(pl.multiple_of(q * high, high), high)
+        return pl.ds(*CHUNKS[q])
+
+    def each_chunk(body):
+        for q in range(len(CHUNKS)):
+            body(q)
 
     def spread(q, plane):
-        for t in range(8):
+        relay_to = jnp.where(opens, 5, 1)
+        for d in (4, 3, 5, 2, 6, 1, 7, 0):
             remote(
-                s_out.at[q], gathered.at[q], plane_send, plane_recv.at[q], 0, plane * 8 + t
+                s_out.at[rows_of(q)], gathered.at[rows_of(q)], plane_send, plane_recv.at[q],
+                relay_to, plane * 8 + lax.rem(z + d, 8),
             ).start()
 
+    @pl.when(solves)
+    def _():
+        self_load.wait()
+        for p in range(4):
+
+            @pl.when(p != y)
+            def _(p=p):
+                landed(own.at[p], own_recv.at[p])
+
+            own_t[:, 128 * p : 128 * (p + 1)] = own[p].T
+
+        own_t[...] = product(own_t[...], inv_hi[1], inv_lo[1], True)
+
     @pl.when(early)
     def _():
-        for p in range(4):
+        for p in (0, 1, 3, 2):
             landed(first.at[p], first_recv.at[p])
             first_t[:, 128 * p : 128 * (p + 1)] = first[p].T
 
     @pl.when(opens)
     def _():
         def open_chunk(q):
-            gathered[q] = product(first_t[rows_of(q)], inv_hi[0], inv_lo[0], True)
-            for t in range(1, 8):
-                remote(
-                    gathered.at[q], gathered.at[q], plane_send, plane_recv.at[q], 4, t
-                ).start()
-
-        each(chunks, open_chunk)
+            s_out[rows_of(q)] = product(first_t[rows_of(q)], inv_hi[0], inv_lo[0], True)
+            spread(q, 0)
+
+        each_chunk(open_chunk)
 
     @pl.when(on_chain)
     def _():
-        @pl.when(z == y + 1)
-        def _():
-            self_load.wait()
-            for p in range(4):
-
-                @pl.when(p != y)
-                def _(p=p):
-                    landed(own.at[p], own_recv.at[p])
-
-                own_t[:, 128 * p : 128 * (p + 1)] = own[p].T
-
         def chain_chunk(q):
+            rows = rows_of(q)
+
             @pl.when(y == 0)
             def _():
-                direct[q] = product(first_t[rows_of(q)], inv_hi[0], inv_lo[0], True)
+                direct[rows] = first_t[rows]
 
             @pl.when(y > 0)
             def _():
-                landed(direct.at[q], direct_recv.at[q])
-
-            u = product(direct[q], f_hi[0], f_lo[0])
+                landed(direct.at[rows], direct_recv.at[q])
+
+            u = product(direct[rows], m_hi[...], m_lo[...])
 
             @pl.when(z > y + 1)
             def _():
-                u_out[q] = u
+                u_out[rows] = u
                 remote(
-                    u_out.at[q], u_in.at[y, q], u_send, u_recv.at[y, q], 0, (z - 1) * 8 + z
+                    u_out.at[rows], u_in.at[y, rows], u_send, u_recv.at[y, q], 0, (z - 1) * 8 + z
                 ).start()
 
             @pl.when(z == y + 1)
             def _():
-                u_out[q] = own_t[rows_of(q)] - u
+                s_out[rows] = own_t[rows] - u
                 for j in range(2):
 
                     @pl.when(j < y)
                     def _(j=j):
-                        landed(u_in.at[j, q], u_recv.at[j, q])
-                        u_out[q] = u_out[q] - u_in[j, q]
-
-                s_out[q] = product(u_out[q], inv_hi[1], inv_lo[1], True)
+                        landed(u_in.at[j, rows], u_recv.at[j, q])
+                        s_out[rows] = s_out[rows] - u_in[j, rows]
+
                 for t in range(2, 4):
 
                     @pl.when(t > z)
                     def _(t=t):
                         remote(
-                            s_out.at[q], direct.at[q], direct_send, direct_recv.at[q], 0, z * 8 + t
+                            s_out.at[rows], direct.at[rows], direct_send, direct_recv.at[q],
+                            0, z * 8 + t,
                         ).start()
 
-                @pl.when(z == 3)
+                @pl.when(z >= 2)
                 def _():
-                    spread(q, 3)
-
-        each(chunks, chain_chunk)
-
-        @pl.when((z == y + 1) & (z < 3))
+                    spread(q, z)
+
+        each_chunk(chain_chunk)
+
+        @pl.when((y == 0) & (z == 1))
         def _():
-            each(chunks, lambda q: spread(q, z))
+            each_chunk(lambda q: spread(q, z))
 
     @pl.when(early)
     def _():
@@ -257,43 +293,40 @@
     keep = jnp.where((row == 0) & (z <= y), 0.0, 1.0).astype(F32)
 
     def plane_chunk(q):
-        @pl.when(jnp.logical_not(opens))
-        def _():
-            landed(gathered.at[q], plane_recv.at[q])
+        rows = rows_of(q)
+
+        landed(gathered.at[rows], plane_recv.at[q])
 
         @pl.when(relays)
         def _():
-            for t in range(1, 8):
+            for d in (3, 5, 4, 6, 1, 2, 7):
                 remote(
-                    gathered.at[q], gathered.at[q], relay_send, plane_recv.at[q],
-                    lax.rem(row + t, 8), col,
+                    gathered.at[rows], gathered.at[rows], relay_send, plane_recv.at[q],
+                    lax.rem(row + d, 8), col,
                 ).start()
 
-        s = gathered[q]
+        s = gathered[rows]
 
         def one(a):
             u = product(s, f_hi[a], f_lo[a])
             u = jnp.where(a == 0, u * keep, u)
             for p in range(4):
-                parts[p, q, a] = u[:, 128 * p : 128 * (p + 1)]
-
-            received[y, q, a] = parts[y, q, a]
-            for d in range(1, 4):
-                to = lax.rem(y + d, 4)
+                parts[p, a, rows] = u[:, 128 * p : 128 * (p + 1)]
+
+            received[y, a, rows] = parts[y, a, rows]
+            for i in range(3):
+                to = lax.rem(y + 1 + lax.rem(i + 1 - lax.rem(y, 2), 3), 4)
                 remote(
-                    parts.at[to, q, a], received.at[y, q, a], part_send, part_recv.at[y, q],
+                    parts.at[to, a, rows], received.at[y, a, rows], part_send, part_recv.at[y, q],
                     row, to * 8 + z,
                 ).start()
 
         each(blocks, one)
 
-    each(chunks, plane_chunk)
+    each_chunk(plane_chunk)
 
     for b in range(4):
-        t = jnp.concatenate(
-            [gathered[q, :, 128 * b : 128 * (b + 1)] for q in range(chunks)], axis=0
-        )
-        turned[b] = t.T
+        turned[b] = gathered[:, 128 * b : 128 * (b + 1)].T
     rows = pl.ds(pl.multiple_of(z * 16, 16), 16)
     for d in range(1, 4):
         to = lax.rem(y + d, 4)
@@ -307,14 +340,14 @@
         def reduce(q, k=k):
             @pl.when(k != y)
             def _():
-                landed(received.at[k, q], part_recv.at[k, q])
+                landed(received.at[k, :, rows_of(q)], part_recv.at[k, q])
 
             def one(a):
-                total[a, rows_of(q)] = total[a, rows_of(q)] - received[k, q, a]
+                total[a, rows_of(q)] = total[a, rows_of(q)] - received[k, a, rows_of(q)]
 
             each(blocks, one)
 
-        each(chunks, reduce)
+        each_chunk(reduce)
 
     for a in range(blocks):
         remaining_out[a] = total[a].T
@@ -354,32 +387,22 @@
             def _(t=t):
                 left(s_out, direct_send)
 
+    @pl.when(solves | opens)
+    def _():
         for t in range(8):
             left(s_out, plane_send)
 
-    @pl.when(opens)
-    def _():
-        for t in range(1, 8):
-            left(gathered, plane_send)
-
-
-def write(solved, remaining, solved_out, remaining_out, sems):
-    copies = [
-        pltpu.make_async_copy(remaining, remaining_out, sems.at[0]),
-        pltpu.make_async_copy(solved, solved_out, sems.at[1]),
-    ]
-    for c in copies:
-        c.start()
-    for c in copies:
-        c.wait()
+
+def write(solved, remaining, solved_out, remaining_out):
+    solved_out[...] = solved[...]
+    remaining_out[...] = remaining[...]
 
 
 def solution(mesh):
     def on_device(factor, rhs, inverses):
         steps = inverses.shape[0]
         blocks, width, nrhs = factor.shape[0], factor.shape[3], rhs.shape[4]
-        chunks = 4
-        high = nrhs // chunks
+        chunks = len(CHUNKS)
         vmem, dma = pltpu.VMEM, pltpu.SemaphoreType.DMA
         shapes = (
             jax.ShapeDtypeStruct((steps, 16, nrhs), F32),
@@ -397,19 +420,22 @@
                 vmem((2, width, width), F32),
                 vmem((2, width, width), BF16),
                 vmem((2, width, width), BF16),
+                vmem((width, width), F32),
+                vmem((width, width), BF16),
+                vmem((width, width), BF16),
                 vmem((blocks, 128, nrhs), F32),
                 vmem((blocks, nrhs, 128), F32),
                 vmem((4, 128, nrhs), F32),
                 vmem((4, 128, nrhs), F32),
                 vmem((nrhs, width), F32),
                 vmem((nrhs, width), F32),
-                vmem((chunks, high, width), F32),
-                vmem((2, chunks, high, width), F32),
-                vmem((chunks, high, width), F32),
-                vmem((chunks, high, width), F32),
-                vmem((chunks, high, width), F32),
-                vmem((4, chunks, blocks, high, 128), F32),
-                vmem((4, chunks, blocks, high, 128), F32),
+                vmem((nrhs, width), F32),
+                vmem((2, nrhs, width), F32),
+                vmem((nrhs, width), F32),
+                vmem((nrhs, width), F32),
+                vmem((nrhs, width), F32),
+                vmem((4, blocks, nrhs, 128), F32),
+                vmem((4, blocks, nrhs, 128), F32),
                 vmem((4, 128, nrhs), F32),
                 vmem((4, 16, nrhs), F32),
                 dma((blocks,)),
@@ -439,9 +465,8 @@
         solved, remaining = pl.pallas_call(
             write,
             out_shape=shapes,
-            in_specs=[pl.BlockSpec(memory_space=pl.ANY)] * 2,
-            out_specs=(pl.BlockSpec(memory_space=pl.ANY),) * 2,
-            scratch_shapes=[dma((2,))],
+            in_specs=[pl.BlockSpec(memory_space=pltpu.VMEM)] * 2,
+            out_specs=(pl.BlockSpec(memory_space=pltpu.VMEM),) * 2,
         )(*results)
         return solved, remaining[:, None, None]
 

time: 70 us -> 53.3 us (0.76)
  the two profiles are of different devices: /device:TPU:101 before, /device:TPU:11 now
where the time goes in v3:
time: 53.3 us; the launch traced here: 53.2 us
  Pallas kernels  52.6 us (99%)
  between operations  0.64 us (1%)
    pallas_call x1, Pallas kernels, on_device(): pl.pallas_call(kernel, out_shape=shapes, in_specs=[pl.BlockSpec(memory_sp...  50.8 us
    pallas_call x1, Pallas kernels, on_device(): pl.pallas_call(write, out_shape=shapes, in_specs=[pl.BlockSpec(memory_spa...  1.79 us

profile of v3, /device:TPU:11, one launch (start us, length us, event | category | flops | bytes accessed | tf_op | source)
XLA Modules:
  0.0 53.2 jit_solution(2693041872013252477)
XLA Ops:
  0.6 50.8 %shard_map.50 = (f32[4,16,128]{2,1,0:T(8,128)}, f32[6,128,128]{2,1,0:T(8,128)}) custom-call(f32[6,1,1,512,512]{4,3,2,1,0:T(8,128)} %factor.1, f32[6,1,1,128,128]{4,3,2,1,0:T(8,128)} %rhs.1, f32[4,512,512]{2,1,0:T(8,128)} %inverses.1), custom_call_target="tpu_custom_call" | custom-call | tf_op jit(solution)/shard_map/pallas_call | solution.py:411
  51.5 1.8 %shard_map.51 = (f32[4,16,128]{2,1,0:T(8,128)}, f32[6,128,128]{2,1,0:T(8,128)}) custom-call(f32[4,16,128]{2,1,0:T(8,128)} %get-tuple-element.6.solved, f32[6,128,128]{2,1,0:T(8,128)} %get-tuple-element.7.remaining), custom_call_target="tpu_custom_call" | custom-call | tf_op jit(solution)/shard_map/pallas_call | solution.py:465

commit v4 on v3

--- a/solution.py
+++ b/solution.py
@@ -393,11 +393,6 @@
             left(s_out, plane_send)
 
 
-def write(solved, remaining, solved_out, remaining_out):
-    solved_out[...] = solved[...]
-    remaining_out[...] = remaining[...]
-
-
 def solution(mesh):
     def on_device(factor, rhs, inverses):
         steps = inverses.shape[0]
@@ -408,9 +403,9 @@
             jax.ShapeDtypeStruct((steps, 16, nrhs), F32),
             jax.ShapeDtypeStruct((blocks, 128, nrhs), F32),
         )
-        results = pl.pallas_call(
+        solved, remaining = pl.pallas_call(
             kernel,
-            out_shape=shapes,
+            out_shape=tuple(vmem(t.shape, t.dtype) for t in shapes),
             in_specs=[pl.BlockSpec(memory_space=pl.ANY)] * 3,
             out_specs=(pl.BlockSpec(memory_space=pltpu.VMEM),) * 2,
             scratch_shapes=[
@@ -462,12 +457,6 @@
                 collective_id=0, has_side_effects=True, vmem_limit_bytes=56 * 2**20
             ),
         )(factor, rhs, inverses)
-        solved, remaining = pl.pallas_call(
-            write,
-            out_shape=shapes,
-            in_specs=[pl.BlockSpec(memory_space=pltpu.VMEM)] * 2,
-            out_specs=(pl.BlockSpec(memory_space=pltpu.VMEM),) * 2,
-        )(*results)
         return solved, remaining[:, None, None]
 
     return jax.shard_map(

time: 53.3 us -> 52.2 us (0.979)
  Pallas kernels: 52.6 us -> 50.1 us
  local copies, waits for them, and re-layouts: 0 us -> 1.36 us
    pallas_call x2 -> x1, Pallas kernels: 52.6 us -> 50.1 us  [on_device(): pl.pallas_call(kernel, out_shape=tuple((vmem(t.shape, t.dtype) for t in s...]
    unnamed x0 -> x2, local copies, waits for them, and re-layouts: none -> 1.36 us
where the time goes in v4:
time: 52.2 us; the launch traced here: 52.1 us
  Pallas kernels  50.1 us (96%)
  local copies, waits for them, and re-layouts  1.36 us (3%)
  between operations  0.64 us (1%)
    pallas_call x1, Pallas kernels, on_device(): pl.pallas_call(kernel, out_shape=tuple((vmem(t.shape, t.dtype) for t in s...  50.1 us
    unnamed x2, local copies, waits for them, and re-layouts  1.36 us

profile of v4, /device:TPU:11, one launch (start us, length us, event | category | flops | bytes accessed | tf_op | source)
XLA Modules:
  0.0 52.1 jit_solution(13283308111105947121)
XLA Ops:
  0.6 50.1 %shard_map.50 = (f32[4,16,128]{2,1,0:T(8,128)S(1)}, f32[6,128,128]{2,1,0:T(8,128)S(1)}) custom-call(f32[6,1,1,512,512]{4,3,2,1,0:T(8,128)} %factor.1, f32[6,1,1,128,128]{4,3,2,1,0:T(8,128)} %rhs.1, f32[4,512,512]{2,1,0:T(8,128)} %inverses.1), custom_call_target="tpu_custom_call" | custom-call | tf_op jit(solution)/shard_map/pallas_call | solution.py:406
  50.7 0.6 %copy.8 = f32[4,16,128]{2,1,0:T(8,128)} copy(f32[4,16,128]{2,1,0:T(8,128)S(1)} %get-tuple-element.8) | data formatting | bytes 65536
  51.3 0.7 %copy.9 = f32[6,1,1,128,128]{4,3,2,1,0:T(8,128)} copy(f32[6,1,1,128,128]{4,3,2,1,0:T(8,128)S(1)} %bitcast.3) | data formatting | bytes 786432
